TPU v7x, 128 devices: a whole 4x4x4 slice. The times are simulated.
128 devices in a mesh: gx: 8 (over y, core), gy: 16 (over z, x).
Axes of the slice: x: 4, y: 4, z: 4, core: 2. Of those that a mesh axis runs over, the one named last changes fastest.
Arguments:
- z_factor: float32 [8, 16, 24, 128, 128], P('gx', 'gy'), may hold values from -1 to 1
- fock: float32 [8, 16, 24, 128, 128], P('gx', 'gy'), may hold values from -1 to 1
- cotangent: float32 [8, 16, 24, 128, 128], P('gx', 'gy'), may hold values from -1 to 1
- tasks_zg: int32 [8, 16, 3, 64], P('gx', 'gy'), may hold values from 0 to 119, as said below
- tasks_fock: int32 [8, 16, 3, 64], P('gx', 'gy'), may hold values from 0 to 119, as said below
- tasks_fz: int32 [8, 16, 3, 64], P('gx', 'gy'), may hold values from 0 to 119, as said below
- tasks_zgt: int32 [8, 16, 3, 64], P('gx', 'gy'), may hold values from 0 to 119, as said below
- tasks_trans: int32 [8, 16, 3, 64], P('gx', 'gy'), may hold values from 0 to 119, as said below
Outputs:
- fock_grad: float32 [8, 16, 24, 128, 128], P('gx', 'gy')
- factor_grad: float32 [8, 16, 24, 128, 128], P('gx', 'gy')
Inputs may be any that keep to these rules, and one draw needn't show every extreme that they name: `tasks_zg`: each cell column's list holds live entries (out below 24) first and then padding entries (out = 24, a = b = 0); out below 24 and a below 24 on live entries, b below 120; the busiest cell column's list is full. `tasks_fock`: each cell column's list holds live entries (out below 24) first and then padding entries (out = 24, a = b = 0); out below 24 and a below 24 on live entries, b below 120; the busiest cell column's list is full. `tasks_fz`: each cell column's list holds live entries (out below 24) first and then padding entries (out = 24, a = b = 0); out below 24 and a below 24 on live entries, b below 120; the busiest cell column's list is full. `tasks_zgt`: each cell column's list holds live entries (out below 24) first and then padding entries (out = 24, a = b = 0); out below 24 and a below 24 on live entries, b below 120; the busiest cell column's list is full. `tasks_trans`: each cell column's list holds live entries (out below 24) first and then padding entries (out = 24, a = b = 0); a and b below 120 and a // 24 = b // 24 on every entry; the busiest cell column's list is full.
All inputs are finite; a program needn't handle non-finite values.
Results may differ from a plain program's by a relative error of at most 0.0003.
Values sent between devices are 32-bit elements; how exact they have to be, the bound alone decides.
A program may use at most 192 MiB of HBM per device.

v0:
```python
import functools

import jax
import jax.numpy as jnp
from jax import lax
from jax.experimental import pallas as pl
from jax.experimental.pallas import tpu as pltpu
from jax.sharding import PartitionSpec as P


TILE = 128
UNROLL = 8
F32 = jnp.float32
I32 = jnp.int32
MESH = pl.DeviceIdType.MESH
STEPS = (("gx", -1), ("gx", 1), ("gy", -1), ("gy", 1))


def split(tile):
    high = tile.astype(jnp.bfloat16)
    low = (tile - high.astype(F32)).astype(jnp.bfloat16)
    return jnp.concatenate([high, low], axis=1)


def product(left, right, turned):
    if turned:
        high, low = right[:, :TILE], right[:, TILE:]
        rows = jnp.concatenate([high, low], axis=0)
        operand = jnp.concatenate([rows, rows], axis=1)
        both = lax.dot_general(left, operand, (((1,), (1,)), ((), ())), preferred_element_type=F32)
    else:
        operand = jnp.concatenate([right, right], axis=0)
        both = lax.dot_general(left, operand, (((1,), (0,)), ((), ())), preferred_element_type=F32)
    return both[:, :TILE] + both[:, TILE:]


def run_list(count, entry, left_of, right_of, turned, total, unroll=UNROLL):
    def step(turn, _):
        entries = [entry(turn * unroll + i) for i in range(unroll)]
        values = [product(left_of(a), right_of(b), turned) for _, a, b in entries]
        for (t, _, _), value in zip(entries, values):
            total[t] += value
        return 0

    lax.fori_loop(0, (count + unroll - 1) // unroll, step, 0)


def live_count(tasks, per_cell):
    length = tasks.shape[2]
    return lax.while_loop(
        lambda n: jnp.logical_and(n < length, tasks[0, 0, jnp.minimum(n, length - 1)] < per_cell),
        lambda n: n + 1,
        jnp.int32(0),
    )


def split_all(source, target, per_cell):
    def step(i, _):
        target[i] = split(source[i])
        return 0

    lax.fori_loop(0, per_cell, step, 0)


def each(count, do):
    def step(i, _):
        do(i)
        return 0

    lax.fori_loop(0, count, step, 0)


def clear(total, first, count):
    def do(i):
        total[first + i] = jnp.zeros(total.shape[1:], total.dtype)

    each(count, do)


def moved_entry(tasks, plan, at):
    return lambda e: (tasks[0, 0, e], tasks[1, 0, e], plan[at, e])


def fetch(sources, grown, sems):
    copies = [
        pltpu.make_async_copy(src, grown.at[pl.ds(at, src.shape[0])], sems.at[i]) for i, (src, at) in enumerate(sources)
    ]
    for c in copies:
        c.start()
    return copies


FOCK_ROW, FZ_ROW, MAP_ROW, ZG_ROW, ZGT_ROW, LIST_ROW, PLAN_ROWS = 0, 1, 2, 6, 7, 8, 32


class Tables:
    def __init__(self, per_cell, length):
        self.per_cell, self.length = per_cell, length
        self.row = lax.broadcasted_iota(I32, (per_cell, length), 0)
        self.lane = lax.broadcasted_iota(I32, (1, TILE), 1)
        self.number = lax.broadcasted_iota(I32, (per_cell, TILE), 0)

    def hits(self, key):
        return jnp.broadcast_to(key, self.row.shape) == self.row

    def named(self, keys, first=0):
        found = sum(self.hits(key).astype(I32) for key in keys)
        found = jnp.where(self.row >= first, found, 0)
        return jnp.minimum(jnp.max(found, axis=1, keepdims=True), 1)

    def of_cell(self, lists, k, first=0):
        return self.named([tasks[2] - k * self.per_cell for tasks in lists], first)

    def inside(self, tasks, k):
        a = tasks[1]
        here = jnp.logical_and(a >= k * self.per_cell, a < (k + 1) * self.per_cell)
        return jnp.logical_and(here, tasks[0] < self.per_cell)

    def outs(self, tasks, k):
        return jnp.where(self.inside(tasks, k), tasks[0], self.per_cell)

    def ranked(self, found):
        square = (self.per_cell, self.per_cell)
        below = (lax.broadcasted_iota(I32, square, 1) < lax.broadcasted_iota(I32, square, 0)).astype(F32)
        return jnp.dot(below, jnp.broadcast_to(found, self.number.shape).astype(F32), preferred_element_type=F32)

    def packed_rows(self, found, first=0):
        spread = jnp.broadcast_to(self.lane - first, self.number.shape).astype(F32)
        here = jnp.logical_and(self.ranked(found) == spread, jnp.broadcast_to(found, self.number.shape) == 1)
        order = jnp.sum(jnp.where(here, self.number, 0), axis=0, keepdims=True)
        return jnp.where(self.lane == TILE - 1, jnp.sum(found), order)

    def rank_of(self, key, found):
        rank = self.ranked(found)[:, : self.length].astype(I32)
        return jnp.sum(jnp.where(self.hits(key), rank, 0), axis=0, keepdims=True)

    def places(self, tasks, lists, first, starts):
        place = tasks[2]
        for k in (3, 4):
            key = tasks[2] - k * self.per_cell
            here = jnp.logical_and(key >= first, key < self.per_cell)
            rank = self.rank_of(key, self.of_cell(lists, k, first))
            place = jnp.where(here, starts[k] + rank, place)
        return place


def by_quarter(lane, values):
    result = values[3]
    for i in (2, 1, 0):
        result = jnp.where(lane < (i + 1) * (TILE // 4), values[i], result)
    return result


def meet_kernel(tzg, tfock, tfz, tzgt, ttrans, g, z, *refs, rooms, lead, cuts):
    ga, tn, gp = refs[:2], refs[2:6], refs[6:8]
    (level, pick, gl, gt, fl, zl, msg, line, lines, picked, source, packed, bulk_s, bulk_r, list_s, list_r) = refs[8:24]
    line_s, line_r, lines_s, lines_r, own, put = refs[24:]
    ny, nx = line.shape[0], lines.shape[0]
    per_cell = g.shape[0]
    ix, iy = lax.axis_index("gx"), lax.axis_index("gy")
    barrier = pltpu.get_barrier_semaphore()
    for j in range(1, nx):
        pl.semaphore_signal(barrier, inc=1, device_id=(lax.rem(ix + j, nx), iy), device_id_type=MESH)
    for j in range(1, ny):
        pl.semaphore_signal(barrier, inc=1, device_id=(ix, lax.rem(iy + j, ny)), device_id_type=MESH)
    rest_g = per_cell - lead
    loads = [
        pltpu.make_async_copy(g.at[pl.ds(lead, rest_g)], source.at[pl.ds(0, rest_g)], own.at[3]),
        pltpu.make_async_copy(z, source.at[pl.ds(rest_g, per_cell)], own.at[4]),
    ]
    for c in loads:
        c.start()
    others = []
    for axis, by in STEPS:
        others.append((lax.rem(ix + by + nx, nx), iy) if axis == "gx" else (ix, lax.rem(iy + by + ny, ny)))
    pl.semaphore_wait(barrier, nx + ny - 2)

    def bulk(i, k, start, size):
        part = pl.ds(start, size)
        return pltpu.make_async_remote_copy(
            g.at[part], ga[(k ^ 1) - 2].at[part], bulk_s.at[i], bulk_r.at[i], device_id=others[k], device_id_type=MESH
        )

    large = [bulk(0, 2, 0, cuts), bulk(1, 3, 0, cuts)]
    for c in large:
        c.start()

    lists = []
    for i in range(2):
        lists += [(tzg, gl.at[i], others[2 + i]), (tzgt, gt.at[i], others[2 + i])]
        lists += [(tfock, fl.at[i], others[2 + i]), (tfz, zl.at[i], others[2 + i])]
    lists += [(ttrans, tn[k], others[k]) for k in range(4)]
    small = []
    for i, (src, dst, to) in enumerate(lists):
        small.append(pltpu.make_async_remote_copy(src, dst, list_s.at[i], list_r.at[i], device_id=to, device_id_type=MESH))
        small[-1].start()

    tables = Tables(per_cell, tfock.shape[2])

    def most(found):
        return functools.reduce(jnp.maximum, [jnp.sum(v) for v in found])

    needs = (
        most([tables.of_cell((tzg, tzgt), k, lead) + tables.of_cell((tfock, tfz), k) for k in (3, 4)]),
        most([tables.named((tables.outs(ttrans, k),)) for k in (1, 2)]),
        most([tables.named((tables.outs(ttrans, k),)) for k in (3, 4)]),
        0,
    )
    msg[...] = by_quarter(tables.lane, needs)
    keep = pltpu.make_async_copy(msg, line.at[pl.ds(0, 1)], own.at[0])
    keep.start()
    keep.wait()
    first = []
    for j in range(1, ny):
        to = (ix, lax.rem(iy + j, ny))
        row = line.at[pl.ds(0, 1)]
        first.append(pltpu.make_async_remote_copy(row, line.at[pl.ds(j, 1)], line_s.at[j], line_r.at[j], device_id=to, device_id_type=MESH))
        first[-1].start()
    rest = [bulk(2, 2, cuts, lead - cuts), bulk(3, 3, cuts, lead - cuts)]
    for c in rest:
        c.start()
    for c in first:
        c.wait()
    keep = pltpu.make_async_copy(line, lines.at[0], own.at[1])
    keep.start()
    second = []
    for j in range(1, nx):
        to = (lax.rem(ix + j, nx), iy)
        second.append(pltpu.make_async_remote_copy(line, lines.at[j], lines_s.at[j], lines_r.at[j], device_id=to, device_id_type=MESH))
        second[-1].start()
    for c in small:
        c.wait()

    pick[...] = jnp.zeros_like(pick)
    for side in range(2):
        g_named = tables.of_cell((gl.at[side], gt.at[side]), 3 + side, lead)
        z_named = tables.of_cell((fl.at[side], zl.at[side]), 3 + side)
        count = jnp.sum(g_named)
        order = jnp.where(tables.lane < count, tables.packed_rows(g_named) - lead, tables.packed_rows(z_named, count) + rest_g)
        pick[side : side + 1, :] = jnp.clip(order, 0, rest_g + per_cell - 1)
    copy = pltpu.make_async_copy(pick, picked, own.at[2])
    copy.start()
    copy.wait()
    for c in loads:
        c.wait()
    puts = []
    for side in range(2):

        def take(s, _, side=side):
            packed[side, s] = source[picked[side, s]]
            return 0

        lax.fori_loop(0, rest_g, take, 0)
        puts.append(pltpu.make_async_copy(packed.at[side], gp[side], put.at[side]))
        puts[-1].start()
    keep.wait()
    for c in second:
        c.wait()
    found = jnp.max(lines[...], axis=0)
    lane = lax.broadcasted_iota(I32, found.shape, 1)
    needs = [jnp.max(jnp.where(by_quarter(lane, [int(i == j) for j in range(4)]) == 1, found, 0)) for i in range(4)]
    first_fit, unfit = 0, jnp.int32(1)
    for level_rooms in rooms[:-1]:
        over = [need > room for need, room in zip(needs, level_rooms)]
        unfit = unfit * functools.reduce(jnp.logical_or, over).astype(I32)
        first_fit = first_fit + unfit
    level[0, 0] = first_fit
    for c in large + rest + puts:
        c.wait()


def pack_kernel(pick, z, out3, out4, packed, put, *, first):
    per_cell, room = z.shape[0], out3.shape[0]
    puts = []
    for side, out in enumerate((out3, out4)):

        def take(s, _, side=side):
            packed[side, s] = z[jnp.clip(pick[side, first + s] - first, 0, per_cell - 1)]
            return 0

        lax.fori_loop(0, room, take, 0)
        puts.append(pltpu.make_async_copy(packed.at[side], out, put.at[side]))
        puts[-1].start()
    for c in puts:
        c.wait()


def run_start(per_cell, lead, k):
    return 3 * per_cell + (k - 3) * (2 * per_cell - lead)


def plan_kernel(tzg, tfock, tfz, tzgt, t0, t1, t2, t3, t4, f, z, plan, fs, ft, zs, table, cut, put, *, lead):
    per_cell, length = f.shape[0], tfock.shape[2]

    def cut_all(i, _):
        tile = f[i]
        cut[0, i] = split(tile)
        cut[1, i] = split(tile.T)
        cut[2, i] = split(z[i])
        return 0

    lax.fori_loop(0, per_cell, cut_all, 0)
    puts = [pltpu.make_async_copy(cut.at[i], out, put.at[i]) for i, out in enumerate((fs, ft, zs))]
    for c in puts:
        c.start()
    tables = Tables(per_cell, length)
    lane = tables.lane
    plan[...] = jnp.zeros_like(plan)
    g_starts = {k: k * per_cell + lead for k in (3, 4)}
    z_starts = {k: run_start(per_cell, lead, k) + jnp.sum(tables.of_cell((tzg, tzgt), k, lead)) for k in (3, 4)}
    for at, tasks, lists, first, starts in (
        (FOCK_ROW, tfock, (tfock, tfz), 0, z_starts),
        (FZ_ROW, tfz, (tfock, tfz), 0, z_starts),
        (ZG_ROW, tzg, (tzg, tzgt), lead, g_starts),
        (ZGT_ROW, tzgt, (tzg, tzgt), lead, g_starts),
    ):
        plan[at : at + 1, pl.ds(0, length)] = tables.places(tasks, lists, first, starts)
    for k in range(1, 5):
        plan[MAP_ROW + k - 1 : MAP_ROW + k, :] = tables.packed_rows(tables.named((tables.outs(t0, k),)))
    square = (length, length)
    before = (lax.broadcasted_iota(I32, square, 0) < lax.broadcasted_iota(I32, square, 1)).astype(F32)
    same = (lax.broadcasted_iota(I32, square, 0) == lax.broadcasted_iota(I32, square, 1)).astype(F32)
    slots = lax.broadcasted_iota(I32, (length, TILE), 1).astype(F32)
    table[...] = jnp.zeros_like(table)
    for k, tasks in enumerate((t0, t1, t2, t3, t4)):
        here, out = tables.inside(tasks, k), tables.outs(tasks, k)
        slot = out if k == 0 else tables.rank_of(out, tables.named((out,)))
        for i, value in enumerate((slot, tasks[1] - k * per_cell, tasks[2] - k * per_cell, here)):
            table[i : i + 1, :] = value.astype(F32)
        earlier = jnp.dot(table[...], before, preferred_element_type=F32)
        table[4:5, :] = earlier[3:4, :]
        turned = lax.dot_general(same, table[...], (((1,), (1,)), ((), ())), preferred_element_type=F32)
        to_slot = jnp.logical_and(jnp.broadcast_to(turned[:, 4:5], slots.shape) == slots, jnp.broadcast_to(turned[:, 3:4], slots.shape) > 0.5)
        moved = jnp.dot(table[...], to_slot.astype(F32), preferred_element_type=F32).astype(I32)
        count = jnp.sum(here.astype(I32))
        at = LIST_ROW + 4 * k
        for i in range(3):
            plan[at + i : at + i + 1, :] = moved[i : i + 1, :]
        plan[at : at + 1, :] = jnp.where(lane < count, moved[0:1, :], TILE - 1)
        plan[at + 3 : at + 4, :] = jnp.where(lane == TILE - 1, count, 0)
    for c in puts:
        c.wait()


def w_kernel(tasks, plan, zs, g0, g1, g2, a3, g3, a4, g4, ws, grown, cut, total, sems, osem):
    per_cell, lead = zs.shape[0], a3.shape[0]
    copies = fetch(g_places(per_cell, lead, g0, g1, g2, a3, g3, a4, g4), grown, sems)
    clear(total, 0, per_cell)
    live = live_count(tasks, per_cell)
    for c in copies:
        c.wait()
    entry = moved_entry(tasks, plan, ZG_ROW)
    run_list(live, entry, lambda a: zs[a], lambda b: split(grown[b]), False, total, 4)
    split_all(total, cut, per_cell)
    out = pltpu.make_async_copy(cut, ws, osem)
    out.start()
    out.wait()


def g_places(per_cell, lead, g0, g1, g2, a3, g3, a4, g4):
    places = [(src, k * per_cell) for k, src in enumerate((g0, g1, g2, a3, a4))]
    return places + [(g3, 3 * per_cell + lead), (g4, 4 * per_cell + lead)]


def p_kernel(plan, ft, ws, p0, p1, p2, p3, p4, total, osem):
    outs = (p0, p1, p2, p3, p4)
    starts = [sum(p.shape[0] for p in outs[:k]) for k in range(6)]
    last = starts[5]

    clear(total, 0, last)

    def one(k, _):
        at = LIST_ROW + 4 * k
        first = sum(jnp.where(k == i, start, 0) for i, start in enumerate(starts[:5]))

        def entry(e):
            return jnp.minimum(first + plan[at, e], last), plan[at + 1, e], plan[at + 2, e]

        run_list(plan[at + 3, TILE - 1], entry, lambda a: ft[a], lambda b: ws[b], False, total, 4)
        return 0

    lax.fori_loop(0, 5, one, 0)
    copies = [pltpu.make_async_copy(total.at[pl.ds(starts[k], p.shape[0])], p, osem.at[k]) for k, p in enumerate(outs)]
    for c in copies:
        c.start()
    for c in copies:
        c.wait()


def rest_kernel(tfock, tfz, tzgt, plan, fs, ws, p0, z0, z1, z2, z3, z4, g0, g1, g2, a3, g3, a4, g4, fock, factor, zgrown, ggrown, us, total, zsem, gsem, osem):
    per_cell, lead = p0.shape[0], a3.shape[0]
    places = [(src, k * per_cell) for k, src in enumerate((z0, z1, z2))]
    for k, first, then in ((3, g3, z3), (4, g4, z4)):
        start = run_start(per_cell, lead, k)
        places += [(first, start), (then, start + first.shape[0])]
    zcopies = fetch(places, zgrown, zsem)
    gcopies = fetch(g_places(per_cell, lead, g0, g1, g2, a3, g3, a4, g4), ggrown, gsem)
    clear(total.at[0], 0, per_cell)
    clear(total.at[1], 0, per_cell)

    def begin(i):
        total[2, i] = p0[i]

    each(per_cell, begin)
    fz_live, fock_live, zgt_live = (live_count(tasks, per_cell) for tasks in (tfz, tfock, tzgt))
    for c in zcopies:
        c.wait()
    run_list(fz_live, moved_entry(tfz, plan, FZ_ROW), lambda a: fs[a], lambda b: split(zgrown[b]), False, total.at[0])
    split_all(total.at[0], us, per_cell)
    run_list(fock_live, moved_entry(tfock, plan, FOCK_ROW), lambda a: ws[a], lambda b: split(zgrown[b]), True, total.at[1])
    out1 = pltpu.make_async_copy(total.at[1, pl.ds(0, per_cell)], fock, osem.at[0])
    out1.start()
    for c in gcopies:
        c.wait()
    run_list(zgt_live, moved_entry(tzgt, plan, ZGT_ROW), lambda a: us[a], lambda b: split(ggrown[b]), True, total.at[2])
    out2 = pltpu.make_async_copy(total.at[2, pl.ds(0, per_cell)], factor, osem.at[1])
    out2.start()
    out1.wait()
    out2.wait()


def join_kernel(plan, part, p1, p2, p3, p4, factor, total, puts, *, pieces):
    per_cell = part.shape[0]
    size = per_cell // pieces
    lists = tuple(enumerate((p1, p2, p3, p4)))
    counts = [jnp.minimum(plan[MAP_ROW + side, TILE - 1], p.shape[0]) for side, p in lists]
    at = [jnp.int32(0)] * len(lists)
    stored = []
    for i in range(pieces):
        piece = pl.ds(i * size, size)

        def begin(t, i=i):
            total[i * size + t] = part[i * size + t]

        each(size, begin)
        for j, (side, p) in enumerate(lists):

            def more(s, j=j, side=side, i=i):
                return jnp.logical_and(s < counts[j], plan[MAP_ROW + side, s] < (i + 1) * size)

            def add(s, side=side, p=p):
                total[plan[MAP_ROW + side, s]] += p[s]
                return s + 1

            at[j] = lax.while_loop(more, add, at[j])
        stored.append(pltpu.make_async_copy(total.at[piece], factor.at[piece], puts.at[i]))
        stored[-1].start()
    for c in stored:
        c.wait()


SMEM = pl.BlockSpec(memory_space=pltpu.SMEM)
VMEM = pl.BlockSpec(memory_space=pltpu.VMEM)
ANY = pl.BlockSpec(memory_space=pl.ANY)
HBM = pl.BlockSpec(memory_space=pltpu.HBM)
DMA = pltpu.SemaphoreType.DMA


def cost(tasks, tiles):
    return pl.CostEstimate(flops=tasks * 2 * TILE**3 * 8, bytes_accessed=tiles * TILE * TILE * 4, transcendentals=0)


def shifted(array, axis, by):
    n = lax.axis_size(axis)
    return lax.ppermute(array, axis, [(i, (i + by) % n) for i in range(n)])


def tiles(n):
    return jax.ShapeDtypeStruct((n, TILE, TILE), F32)


def cut_tiles(n):
    return jax.ShapeDtypeStruct((n, TILE, 2 * TILE), jnp.bfloat16)


def join(plan, part, sums):
    per_cell = part.shape[0]
    pieces = 2 if per_cell % 2 == 0 else 1
    return pl.pallas_call(
        functools.partial(join_kernel, pieces=pieces),
        name="join_kernel",
        out_shape=pltpu.HBM((per_cell, TILE, TILE), F32),
        in_specs=[SMEM] + [VMEM] * 5,
        out_specs=HBM,
        scratch_shapes=[pltpu.VMEM((per_cell, TILE, TILE), F32), DMA((pieces,))],
        compiler_params=pltpu.CompilerParams(vmem_limit_bytes=16 * 2**20),
        cost_estimate=cost(0, 4 * per_cell),
    )(plan, part, *sums)


def finish(run_room, x_room, y_room, gp, z, f, g, tzg, tfock, tfz, tzgt, ttrans, tn, pick, ga):
    per_cell = z.shape[0]
    cap = tzg.shape[2]
    grown = pltpu.VMEM((5 * per_cell, TILE, TILE), F32)
    cut = pltpu.VMEM((per_cell, TILE, 2 * TILE), jnp.bfloat16)
    params = pltpu.CompilerParams(vmem_limit_bytes=40 * 2**20)
    gy = (shifted(gp[0], "gy", 1), shifted(gp[1], "gy", -1))
    first = gp[0].shape[0]
    z_room = run_room - first
    pack = pl.pallas_call(
        functools.partial(pack_kernel, first=first),
        name="pack_kernel",
        out_shape=[tiles(z_room)] * 2,
        in_specs=[SMEM, VMEM],
        out_specs=[ANY] * 2,
        scratch_shapes=[pltpu.VMEM((2, z_room, TILE, TILE), F32), DMA((2,))],
        compiler_params=pltpu.CompilerParams(vmem_limit_bytes=16 * 2**20),
        cost_estimate=cost(0, 4 * per_cell),
    )
    z3, z4 = pack(pick, z)
    g_late, z_late, z3, z4 = lax.optimization_barrier((g, z, z3, z4))
    gn = (shifted(g_late, "gx", 1), shifted(g_late, "gx", -1), ga[0], gy[0], ga[1], gy[1])
    zy = (shifted(z3, "gy", 1), shifted(z4, "gy", -1))
    zn = (shifted(z_late, "gx", 1), shifted(z_late, "gx", -1)) + zy
    make_plan = pl.pallas_call(
        functools.partial(plan_kernel, lead=ga[0].shape[0]),
        name="plan_kernel",
        out_shape=[jax.ShapeDtypeStruct((PLAN_ROWS, TILE), I32)] + [cut_tiles(per_cell)] * 3,
        in_specs=[VMEM] * 11,
        out_specs=[VMEM] + [ANY] * 3,
        scratch_shapes=[pltpu.VMEM((8, cap), F32), pltpu.VMEM((3, per_cell, TILE, 2 * TILE), jnp.bfloat16), DMA((3,))],
        compiler_params=pltpu.CompilerParams(vmem_limit_bytes=24 * 2**20),
        cost_estimate=cost(cap, 8 * per_cell),
    )
    plan, fs, ft, zs = make_plan(tzg, tfock, tfz, tzgt, ttrans, *tn, f, z)
    ws = pl.pallas_call(
        w_kernel,
        name="w_kernel",
        out_shape=cut_tiles(per_cell),
        in_specs=[SMEM, SMEM, VMEM] + [ANY] * 7,
        out_specs=ANY,
        scratch_shapes=[grown, cut, pltpu.VMEM((per_cell + 1, TILE, TILE), F32), DMA((7,)), DMA],
        compiler_params=params,
        cost_estimate=cost(cap, 7 * per_cell),
    )(tzg, plan, zs, g, *gn)
    p = pl.pallas_call(
        p_kernel,
        name="p_kernel",
        out_shape=[tiles(n) for n in (per_cell, x_room, x_room, y_room, y_room)],
        in_specs=[SMEM] + [VMEM] * 2,
        out_specs=[ANY] * 5,
        scratch_shapes=[pltpu.VMEM((per_cell + 2 * x_room + 2 * y_room + 1, TILE, TILE), F32), DMA((5,))],
        compiler_params=params,
        cost_estimate=cost(2 * cap, 7 * per_cell),
    )(plan, ft, ws)
    pn = []
    for k, (axis, by) in enumerate(STEPS):
        pn.append(shifted(p[k + 1], axis, -by))
    fock_grad, part = pl.pallas_call(
        rest_kernel,
        name="rest_kernel",
        out_shape=[pltpu.HBM((per_cell, TILE, TILE), F32), tiles(per_cell)],
        in_specs=[SMEM] * 4 + [VMEM] * 3 + [ANY] * 12,
        out_specs=[HBM, ANY],
        scratch_shapes=[
            pltpu.VMEM((run_start(per_cell, ga[0].shape[0], 5), TILE, TILE), F32),
            grown,
            cut,
            pltpu.VMEM((3, per_cell + 1, TILE, TILE), F32),
            DMA((7,)),
            DMA((7,)),
            DMA((2,)),
        ],
        compiler_params=params,
        cost_estimate=cost(3 * cap, 14 * per_cell),
    )(tfock, tfz, tzgt, plan, fs, ws, p[0], z, *zn, g, *gn)
    return fock_grad, join(plan, part, pn)


def rooms_of(per_cell, lead):
    levels = ((29, 18, 12), (29, 18, 14), (30, 18, 13), (31, 18, 15), (34, 18, 17))
    scaled = [tuple(per_cell * room // 24 for room in level) for level in levels]
    return scaled + [(2 * per_cell - lead, per_cell, per_cell)]


def body(z_factor, fock, cotangent, tasks_zg, tasks_fock, tasks_fz, tasks_zgt, tasks_trans):
    per_cell = z_factor.shape[2]
    nx, ny = lax.axis_size("gx"), lax.axis_size("gy")
    z, f, g = z_factor[0, 0], fock[0, 0], cotangent[0, 0]
    lists = (tasks_zg, tasks_fock, tasks_fz, tasks_zgt, tasks_trans)
    tzg, tfock, tfz, tzgt, ttrans = (t.reshape(t.shape[2], 1, t.shape[3]) for t in lists)
    a_list = jax.ShapeDtypeStruct(tzg.shape, I32)
    lead = per_cell // 3
    rooms = rooms_of(per_cell, lead)
    met = pl.pallas_call(
        functools.partial(meet_kernel, rooms=rooms, lead=lead, cuts=lead // 4),
        name="meet_kernel",
        out_shape=[tiles(lead)] * 2
        + [a_list] * 4
        + [tiles(per_cell - lead)] * 2
        + [jax.ShapeDtypeStruct((1, 1), I32), jax.ShapeDtypeStruct((8, TILE), I32)],
        in_specs=[VMEM] * 5 + [ANY] * 2,
        out_specs=[ANY] * 2 + [VMEM] * 4 + [ANY] * 2 + [SMEM, VMEM],
        scratch_shapes=[pltpu.VMEM((2,) + tzg.shape, I32)] * 4
        + [
            pltpu.VMEM((1, TILE), I32),
            pltpu.VMEM((ny, TILE), I32),
            pltpu.VMEM((nx, ny, TILE), I32),
            pltpu.SMEM((8, TILE), I32),
            pltpu.VMEM((2 * per_cell - lead, TILE, TILE), F32),
            pltpu.VMEM((2, per_cell - lead, TILE, TILE), F32),
            DMA((4,)),
            DMA((4,)),
            DMA((12,)),
            DMA((12,)),
            DMA((ny,)),
            DMA((ny,)),
            DMA((nx,)),
            DMA((nx,)),
            DMA((5,)),
            DMA((2,)),
        ],
        compiler_params=pltpu.CompilerParams(collective_id=0, has_side_effects=True),
    )(tzg, tfock, tfz, tzgt, ttrans, g, z)
    ga, tn, gp, level, pick = met[:2], met[2:6], met[6:8], met[8], met[9]
    operands = (gp, z, f, g, tzg, tfock, tfz, tzgt, ttrans, tn, pick, ga)
    fock_grad, factor_grad = lax.switch(level[0, 0], [functools.partial(finish, *room) for room in rooms], *operands)
    return fock_grad[None, None], factor_grad[None, None]


def solution(mesh):
    cells = P("gx", "gy", None, None, None)
    lists = P("gx", "gy", None, None)
    return jax.shard_map(
        body,
        mesh=mesh,
        in_specs=(cells,) * 3 + (lists,) * 5,
        out_specs=(cells, cells),
        check_vma=False,
    )
```

profile of v0, /device:TPU:0, one launch (start us, length us, event | category | flops | bytes accessed | tf_op | source)
XLA Modules:
  0.0 118.5 jit_solution(14930904539144139658)
XLA Ops:
  0.7 24.4 %meet_kernel.1 = (f32[8,128,128]{2,1,0:T(8,128)S(1)}, f32[8,128,128]{2,1,0:T(8,128)S(1)}, s32[3,1,64]{2,1,0:T(1,128)S(1)}, s32[3,1,64]{2,1,0:T(1,128)S(1)}, s32[...) custom-call(s32[3,1,64]{2,1,0:T(1,128)} %bitcast.22, ...), custom_call_target="tpu_custom_call" | custom-call | tf_op jit(solution)/shard_map/meet_kernel/pallas_call | solution.py:585
  25.7 92.5 %conditional.1 = (f32[24,128,128]{2,1,0:T(8,128)}, f32[1,1,24,128,128]{4,3,2,1,0:T(8,128)}) conditional(s32[]{:T(128)} %bitcast.13, (s32[3,1,64]{2,1,0:T(1,128)S(1)}, s32[3,1,64]{2,1,0:T(1,128)S(1)}, s32[3,1,64]{2,1,0:T(1,128)S(1)}, s32[3,1,64]{2,1,0:T(1,128)S(1)}, s32[3,1,64]{2,1,0:T(1,128)S(1)}, ...), branch_computations={%region_0.0_spmd, %region_1.0_spmd, %region_2.0_spmd, %region_3.0_... | conditional | flops 15032385536 | bytes 211813168 | solution.py:617
  26.0 0.0 copy-start.47
  26.0 2.5 %pack_kernel.8 = (f32[14,128,128]{2,1,0:T(8,128)S(1)}, f32[14,128,128]{2,1,0:T(8,128)S(1)}) custom-call(s32[8,128]{1,0:T(8,128)S(1)} %get-tuple-element.288.pick, f32[24,128,128]{2,1,0:T(8,128)} %get-tuple-element.298.z.z0), custom_call_target="tpu_custom_call" | custom-call | bytes 6291456 | tf_op jit(solution)/shard_map/cond/branch_2_fun/pack_kernel/pallas_call | solution.py:510
  28.5 0.0 collective-permute-start.25
  28.5 0.5 collective-permute-start.24
  29.0 5.3 %collective-permute-start.27 = (f32[16,128,128]{2,1,0:T(8,128)}, f32[16,128,128]{2,1,0:T(8,128)S(1)}, u32[]{:S(2)}, u32[]{:S(2)}) collective-permute-start(f32[16,128,128]{2,1,0:T(8,128)} %get-tuple-element.295), channel_id=1, source_target_pairs={{0,15},{1,0},{2,1},{3,2},{4,3},{5,4},{6,5},{7,6},{8,7},{9,8},{10,9... | collective-permute-start | bytes 3145736 | tf_op jit(solution)/shard_map/cond/branch_2_fun/ppermute | solution.py:465
  34.3 1.9 %collective-permute-start.29 = (f32[24,128,128]{2,1,0:T(8,128)}, f32[24,128,128]{2,1,0:T(8,128)S(1)}, u32[]{:S(2)}, u32[]{:S(2)}) collective-permute-start(f32[24,128,128]{2,1,0:T(8,128)} %get-tuple-element.298.z.z0), channel_id=1, source_target_pairs={{0,112},{16,0},{32,16},{48,32},{64,48},{80,64},{96,80},{112,96},{1... | collective-permute-start | bytes 4718600 | tf_op jit(solution)/shard_map/cond/branch_2_fun/ppermute | solution.py:465
  36.3 21.9 %collective-permute-done.26.g3 = f32[16,128,128]{2,1,0:T(8,128)S(1)} collective-permute-done((f32[16,128,128]{2,1,0:T(8,128)S(1)}, f32[16,128,128]{2,1,0:T(8,128)S(1)}, u32[]{:S(2)}, u32[]{:S(2)}) %collective-permute-start.26) | collective-permute-done | bytes 1048608 | tf_op jit(solution)/shard_map/cond/branch_2_fun/ppermute | solution.py:465
  58.2 5.9 %plan_kernel.8 = (s32[32,128]{1,0:T(8,128)S(1)}, bf16[24,128,256]{2,1,0:T(8,128)(2,1)S(1)}, bf16[24,128,256]{2,1,0:T(8,128)(2,1)S(1)}, bf16[24,128,256]{2,1,0:T(8,128)(2,1)S(1)}) custom-call(s32[3,1,64]{2,1,0:T(1,128)S(1)} %get-tuple-element.276.tzg.tasks, s32[3,1,64]{2,1,0:T(1,128)S(1)} %get-tuple-element.273.tfock, ...), custom_call_target="tpu_custom_call" | custom-call | flops 2147483648 | bytes 12582912 | tf_op jit(solution)/shard_map/cond/branch_2_fun/plan_kernel/pallas_call | solution.py:525
  64.1 1.1 copy-done.30
  65.2 5.3 %collective-permute-start.31 = (f32[14,128,128]{2,1,0:T(8,128)S(1)}, f32[14,128,128]{2,1,0:T(8,128)S(1)}, u32[]{:S(2)}, u32[]{:S(2)}) collective-permute-start(f32[14,128,128]{2,1,0:T(8,128)S(1)} %get-tuple-element.300), channel_id=1, source_target_pairs={{0,15},{1,0},{2,1},{3,2},{4,3},{5,4},{6,5},{7,6},{8,7},{9,8},{10,9... | collective-permute-start | bytes 2752520 | tf_op jit(solution)/shard_map/cond/branch_2_fun/ppermute | solution.py:465
  70.6 5.2 %w_kernel.8.ws = bf16[24,128,256]{2,1,0:T(8,128)(2,1)S(1)} custom-call(s32[3,1,64]{2,1,0:T(1,128)S(1)} %get-tuple-element.276.tzg.tasks, s32[32,128]{1,0:T(8,128)S(1)} %get-tuple-element.284.plan, bf16[24,128,256]{2,1,0:T(8,128)(2,1)S(1)} %get-tuple-element.286.zs, f32[24,128,128]{2,1,0:T(8,128)} %get-tuple-element.291.g0, ...), custom_call_target="tpu_custom_call" | custom-call | flops 2147483648 | bytes 11010048 | tf_op jit(solution)/shard_map/cond/branch_2_fun/w_kernel/pallas_call | solution.py:526
  75.8 4.6 %p_kernel.8 = (f32[24,128,128]{2,1,0:T(8,128)S(1)}, f32[18,128,128]{2,1,0:T(8,128)S(1)}, f32[18,128,128]{2,1,0:T(8,128)S(1)}, f32[13,128,128]{2,1,0:T(8,128)S(1)}, f32[13,128,128]{2,1,0:T(8,128)S(1)}) custom-call(s32[32,128]{1,0:T(8,128)S(1)} %get-tuple-element.284.plan, bf16[24,128,256]{2,1,0:T(8,128)(2,1)S(1)} %get-tuple-element.296.ft, ...), custom_call_target="tpu_custom_call" | custom-call | flops 4294967296 | bytes 11010048 | tf_op jit(solution)/shard_map/cond/branch_2_fun/p_kernel/pallas_call | solution.py:536
  80.5 1.1 copy-done.32
  81.6 2.9 %collective-permute-done.30.z3 = f32[14,128,128]{2,1,0:T(8,128)S(1)} collective-permute-done((f32[14,128,128]{2,1,0:T(8,128)S(1)}, f32[14,128,128]{2,1,0:T(8,128)S(1)}, u32[]{:S(2)}, u32[]{:S(2)}) %collective-permute-start.30) | collective-permute-done | bytes 917536 | tf_op jit(solution)/shard_map/cond/branch_2_fun/ppermute | solution.py:465
  84.5 0.7 collective-permute-start.33
  85.2 5.6 %collective-permute-done.31.z4 = f32[14,128,128]{2,1,0:T(8,128)S(1)} collective-permute-done((f32[14,128,128]{2,1,0:T(8,128)S(1)}, f32[14,128,128]{2,1,0:T(8,128)S(1)}, u32[]{:S(2)}, u32[]{:S(2)}) %collective-permute-start.31) | collective-permute-done | bytes 917536 | tf_op jit(solution)/shard_map/cond/branch_2_fun/ppermute | solution.py:465
  90.8 5.8 %collective-permute-start.35 = (f32[13,128,128]{2,1,0:T(8,128)S(1)}, f32[13,128,128]{2,1,0:T(8,128)S(1)}, u32[]{:S(2)}, u32[]{:S(2)}) collective-permute-start(f32[13,128,128]{2,1,0:T(8,128)S(1)} %get-tuple-element.306), channel_id=1, source_target_pairs={{0,15},{1,0},{2,1},{3,2},{4,3},{5,4},{6,5},{7,6},{8,7},{9,8},{10,9... | collective-permute-start | bytes 2555912 | tf_op jit(solution)/shard_map/cond/branch_2_fun/ppermute | solution.py:465
  96.6 1.4 %copy-done.31 = bf16[24,128,256]{2,1,0:T(8,128)(2,1)S(1)} copy-done((bf16[24,128,256]{2,1,0:T(8,128)(2,1)S(1)}, bf16[24,128,256]{2,1,0:T(8,128)(2,1)}, u32[]{:S(2)}) %copy-start.31) | copy-done | bytes 1572888 | tf_op jit(solution)/shard_map/cond
  98.1 1.4 %copy-done.33 = f32[24,128,128]{2,1,0:T(8,128)S(1)} copy-done((f32[24,128,128]{2,1,0:T(8,128)S(1)}, f32[24,128,128]{2,1,0:T(8,128)}, u32[]{:S(2)}) %copy-start.33) | copy-done | bytes 1572888 | tf_op jit(solution)/shard_map/cond
  99.5 10.9 %rest_kernel.8 = (f32[24,128,128]{2,1,0:T(8,128)}, f32[24,128,128]{2,1,0:T(8,128)S(1)}) custom-call(s32[3,1,64]{2,1,0:T(1,128)S(1)} %get-tuple-element.273.tfock, s32[3,1,64]{2,1,0:T(1,128)S(1)} %get-tuple-element.274.tfz, s32[3,1,64]{2,1,0:T(1,128)S(1)} %get-tuple-element.275.tzgt, s32[32,128]{1,0:T(8,128)S(1)} %get-tuple-element.284.plan, ...), custom_call_target="tpu_custom_call" | custom-call | flops 6442450944 | bytes 22020096 | tf_op jit(solution)/shard_map/cond/branch_2_fun/rest_kernel/pallas_call | solution.py:549
  110.3 5.1 %collective-permute-done.34.p3 = f32[13,128,128]{2,1,0:T(8,128)S(1)} collective-permute-done((f32[13,128,128]{2,1,0:T(8,128)S(1)}, f32[13,128,128]{2,1,0:T(8,128)S(1)}, u32[]{:S(2)}, u32[]{:S(2)}) %collective-permute-start.34) | collective-permute-done | bytes 852000 | tf_op jit(solution)/shard_map/cond/branch_2_fun/ppermute | solution.py:465
  115.4 2.3 %join_kernel.8 = f32[24,128,128]{2,1,0:T(8,128)} custom-call(s32[32,128]{1,0:T(8,128)S(1)} %get-tuple-element.284.plan, f32[24,128,128]{2,1,0:T(8,128)S(1)} %get-tuple-element.302.part, f32[18,128,128]{2,1,0:T(8,128)S(1)} %collective-permute-done.32.p1, f32[18,128,128]{2,1,0:T(8,128)S(1)} %collective-permute-done.33.p2, ...), custom_call_target="tpu_custom_call" | custom-call | bytes 6291456 | tf_op jit(solution)/shard_map/cond/branch_2_fun/join_kernel/pallas_call | solution.py:479
  (36 shorter events, 0.1 us)
Async XLA Ops:
  0.6 25.1 %copy-start.40 = (s32[1,1,3,64]{3,1,2,0:T(1,128)S(1)}, s32[1,1,3,64]{3,1,2,0:T(1,128)}, u32[]{:S(2)}) copy-start(s32[1,1,3,64]{3,1,2,0:T(1,128)} %param.17) | copy-start | bytes 2308
  0.6 25.1 %copy-start.41 = (s32[1,1,3,64]{3,1,2,0:T(1,128)S(1)}, s32[1,1,3,64]{3,1,2,0:T(1,128)}, u32[]{:S(2)}) copy-start(s32[1,1,3,64]{3,1,2,0:T(1,128)} %param.18) | copy-start | bytes 2308
  0.7 25.1 %copy-start.42 = (s32[1,1,3,64]{3,1,2,0:T(1,128)S(1)}, s32[1,1,3,64]{3,1,2,0:T(1,128)}, u32[]{:S(2)}) copy-start(s32[1,1,3,64]{3,1,2,0:T(1,128)} %param.19) | copy-start | bytes 2308
  0.7 25.1 %copy-start.43 = (s32[1,1,3,64]{3,1,2,0:T(1,128)S(1)}, s32[1,1,3,64]{3,1,2,0:T(1,128)}, u32[]{:S(2)}) copy-start(s32[1,1,3,64]{3,1,2,0:T(1,128)} %param.20) | copy-start | bytes 2308
  0.7 25.1 %copy-start.44 = (s32[1,1,3,64]{3,1,2,0:T(1,128)S(1)}, s32[1,1,3,64]{3,1,2,0:T(1,128)}, u32[]{:S(2)}) copy-start(s32[1,1,3,64]{3,1,2,0:T(1,128)} %param.21) | copy-start | bytes 2308
  25.9 44.6 %copy-start.36 = (f32[8,128,128]{2,1,0:T(8,128)}, f32[8,128,128]{2,1,0:T(8,128)S(1)}, u32[]{:S(2)}) copy-start(f32[8,128,128]{2,1,0:T(8,128)S(1)} %get-tuple-element.294.a4) | copy-start | bytes 1572868 | tf_op jit(solution)/shard_map/cond
  26.0 32.2 %copy-start.47 = (f32[24,128,128]{2,1,0:T(8,128)S(1)}, f32[24,128,128]{2,1,0:T(8,128)}, u32[]{:S(2)}) copy-start(f32[24,128,128]{2,1,0:T(8,128)} %get-tuple-element.282.f) | copy-start | bytes 4718596 | tf_op jit(solution)/shard_map/cond
  28.5 36.7 %collective-permute-start.25 = (f32[24,128,128]{2,1,0:T(8,128)}, f32[24,128,128]{2,1,0:T(8,128)S(1)}, u32[]{:S(2)}, u32[]{:S(2)}) collective-permute-start(f32[24,128,128]{2,1,0:T(8,128)} %get-tuple-element.291.g0), channel_id=1, source_target_pairs={{0,112},{16,0},{32,16},{48,32},{64,48},{80,64},{96,80},{112,96},{1... | collective-permute-start | bytes 4718600 | tf_op jit(solution)/shard_map/cond/branch_2_fun/ppermute | solution.py:465
  28.5 42.1 %collective-permute-start.24 = (f32[24,128,128]{2,1,0:T(8,128)}, f32[24,128,128]{2,1,0:T(8,128)S(1)}, u32[]{:S(2)}, u32[]{:S(2)}) collective-permute-start(f32[24,128,128]{2,1,0:T(8,128)} %get-tuple-element.291.g0), channel_id=1, source_target_pairs={{0,16},{16,32},{32,48},{48,64},{64,80},{80,96},{96,112},{112,0},{1... | collective-permute-start | bytes 4718600 | tf_op jit(solution)/shard_map/cond/branch_2_fun/ppermute | solution.py:465
  29.0 29.2 %collective-permute-start.26 = (f32[16,128,128]{2,1,0:T(8,128)S(1)}, f32[16,128,128]{2,1,0:T(8,128)S(1)}, u32[]{:S(2)}, u32[]{:S(2)}) collective-permute-start(f32[16,128,128]{2,1,0:T(8,128)S(1)} %get-tuple-element.293), channel_id=1, source_target_pairs={{0,1},{1,2},{2,3},{3,4},{4,5},{5,6},{6,7},{7,8},{8,9},{9,10},{10,1... | collective-permute-start | bytes 3145736 | tf_op jit(solution)/shard_map/cond/branch_2_fun/ppermute | solution.py:465
  29.0 29.2 %collective-permute-start.27 = (f32[16,128,128]{2,1,0:T(8,128)}, f32[16,128,128]{2,1,0:T(8,128)S(1)}, u32[]{:S(2)}, u32[]{:S(2)}) collective-permute-start(f32[16,128,128]{2,1,0:T(8,128)} %get-tuple-element.295), channel_id=1, source_target_pairs={{0,15},{1,0},{2,1},{3,2},{4,3},{5,4},{6,5},{7,6},{8,7},{9,8},{10,9... | collective-permute-start | bytes 3145736 | tf_op jit(solution)/shard_map/cond/branch_2_fun/ppermute | solution.py:465
  34.3 56.5 %collective-permute-start.29 = (f32[24,128,128]{2,1,0:T(8,128)}, f32[24,128,128]{2,1,0:T(8,128)S(1)}, u32[]{:S(2)}, u32[]{:S(2)}) collective-permute-start(f32[24,128,128]{2,1,0:T(8,128)} %get-tuple-element.298.z.z0), channel_id=1, source_target_pairs={{0,112},{16,0},{32,16},{48,32},{64,48},{80,64},{96,80},{112,96},{1... | collective-permute-start | bytes 4718600 | tf_op jit(solution)/shard_map/cond/branch_2_fun/ppermute | solution.py:465
  58.2 38.5 %collective-permute-start.28 = (f32[24,128,128]{2,1,0:T(8,128)}, f32[24,128,128]{2,1,0:T(8,128)S(1)}, u32[]{:S(2)}, u32[]{:S(2)}) collective-permute-start(f32[24,128,128]{2,1,0:T(8,128)} %get-tuple-element.298.z.z0), channel_id=1, source_target_pairs={{0,16},{16,32},{32,48},{48,64},{64,80},{80,96},{96,112},{112,0},{1... | collective-permute-start | bytes 4718600 | tf_op jit(solution)/shard_map/cond/branch_2_fun/ppermute | solution.py:465
  58.2 26.4 %collective-permute-start.30 = (f32[14,128,128]{2,1,0:T(8,128)S(1)}, f32[14,128,128]{2,1,0:T(8,128)S(1)}, u32[]{:S(2)}, u32[]{:S(2)}) collective-permute-start(f32[14,128,128]{2,1,0:T(8,128)S(1)} %get-tuple-element.299), channel_id=1, source_target_pairs={{0,1},{1,2},{2,3},{3,4},{4,5},{5,6},{6,7},{7,8},{8,9},{9,10},{10,1... | collective-permute-start | bytes 2752520 | tf_op jit(solution)/shard_map/cond/branch_2_fun/ppermute | solution.py:465
  65.2 10.6 %copy-start.2 = (f32[24,128,128]{2,1,0:T(8,128)}, f32[24,128,128]{2,1,0:T(8,128)S(1)}, u32[]{:S(2)}) copy-start(f32[24,128,128]{2,1,0:T(8,128)S(1)} %collective-permute-done.25.g2) | copy-start | bytes 4718596 | tf_op jit(solution)/shard_map/cond
  65.2 25.6 %collective-permute-start.31 = (f32[14,128,128]{2,1,0:T(8,128)S(1)}, f32[14,128,128]{2,1,0:T(8,128)S(1)}, u32[]{:S(2)}, u32[]{:S(2)}) collective-permute-start(f32[14,128,128]{2,1,0:T(8,128)S(1)} %get-tuple-element.300), channel_id=1, source_target_pairs={{0,15},{1,0},{2,1},{3,2},{4,3},{5,4},{6,5},{7,6},{8,7},{9,8},{10,9... | collective-permute-start | bytes 2752520 | tf_op jit(solution)/shard_map/cond/branch_2_fun/ppermute | solution.py:465
  70.5 5.3 %copy-start.7 = (f32[24,128,128]{2,1,0:T(8,128)}, f32[24,128,128]{2,1,0:T(8,128)S(1)}, u32[]{:S(2)}) copy-start(f32[24,128,128]{2,1,0:T(8,128)S(1)} %collective-permute-done.24.g1) | copy-start | bytes 4718596 | tf_op jit(solution)/shard_map/cond
  75.8 20.8 %copy-start.37 = (f32[8,128,128]{2,1,0:T(8,128)S(1)}, f32[8,128,128]{2,1,0:T(8,128)}, u32[]{:S(2)}) copy-start(f32[8,128,128]{2,1,0:T(8,128)} %copy-done.36) | copy-start | bytes 1572868 | tf_op jit(solution)/shard_map/cond
  81.6 33.8 %collective-permute-start.32 = (f32[18,128,128]{2,1,0:T(8,128)S(1)}, f32[18,128,128]{2,1,0:T(8,128)S(1)}, u32[]{:S(2)}, u32[]{:S(2)}) collective-permute-start(f32[18,128,128]{2,1,0:T(8,128)S(1)} %get-tuple-element.303), channel_id=1, source_target_pairs={{0,16},{16,32},{32,48},{48,64},{64,80},{80,96},{96,112},{112,0},{1... | collective-permute-start | bytes 3538952 | tf_op jit(solution)/shard_map/cond/branch_2_fun/ppermute | solution.py:465
  84.5 30.9 %collective-permute-start.33 = (f32[18,128,128]{2,1,0:T(8,128)S(1)}, f32[18,128,128]{2,1,0:T(8,128)S(1)}, u32[]{:S(2)}, u32[]{:S(2)}) collective-permute-start(f32[18,128,128]{2,1,0:T(8,128)S(1)} %get-tuple-element.304), channel_id=1, source_target_pairs={{0,112},{16,0},{32,16},{48,32},{64,48},{80,64},{96,80},{112,96},{1... | collective-permute-start | bytes 3538952 | tf_op jit(solution)/shard_map/cond/branch_2_fun/ppermute | solution.py:465
  90.8 24.6 %collective-permute-start.34 = (f32[13,128,128]{2,1,0:T(8,128)S(1)}, f32[13,128,128]{2,1,0:T(8,128)S(1)}, u32[]{:S(2)}, u32[]{:S(2)}) collective-permute-start(f32[13,128,128]{2,1,0:T(8,128)S(1)} %get-tuple-element.305), channel_id=1, source_target_pairs={{0,1},{1,2},{2,3},{3,4},{4,5},{5,6},{6,7},{7,8},{8,9},{9,10},{10,1... | collective-permute-start | bytes 2555912 | tf_op jit(solution)/shard_map/cond/branch_2_fun/ppermute | solution.py:465
  90.8 24.6 %collective-permute-start.35 = (f32[13,128,128]{2,1,0:T(8,128)S(1)}, f32[13,128,128]{2,1,0:T(8,128)S(1)}, u32[]{:S(2)}, u32[]{:S(2)}) collective-permute-start(f32[13,128,128]{2,1,0:T(8,128)S(1)} %get-tuple-element.306), channel_id=1, source_target_pairs={{0,15},{1,0},{2,1},{3,2},{4,3},{5,4},{6,5},{7,6},{8,7},{9,8},{10,9... | collective-permute-start | bytes 2555912 | tf_op jit(solution)/shard_map/cond/branch_2_fun/ppermute | solution.py:465
  96.6 1.4 %copy-start.31 = (bf16[24,128,256]{2,1,0:T(8,128)(2,1)S(1)}, bf16[24,128,256]{2,1,0:T(8,128)(2,1)}, u32[]{:S(2)}) copy-start(bf16[24,128,256]{2,1,0:T(8,128)(2,1)} %copy-done.30) | copy-start | bytes 4718596 | tf_op jit(solution)/shard_map/cond
  98.1 1.4 %copy-start.33 = (f32[24,128,128]{2,1,0:T(8,128)S(1)}, f32[24,128,128]{2,1,0:T(8,128)}, u32[]{:S(2)}) copy-start(f32[24,128,128]{2,1,0:T(8,128)} %copy-done.32) | copy-start | bytes 4718596 | tf_op jit(solution)/shard_map/cond
  (2 other events, 2.3 us)
where the time goes:
time: 119 us; the launch traced here: 118 us
  Pallas kernels  55.8 us (47%)
  waiting for transfers between devices  35.5 us (30%)
  starting transfers between devices  19.6 us (16%)
  local copies, waits for them, and re-layouts  5.13 us (4%)
  between operations  1.57 us (1%)
    ppermute x12, waiting for transfers between devices, shifted(): return lax.ppermute(array, axis, [(i, (i + by) % n) for i in range(n)])  35.5 us
    pallas_call x1, Pallas kernels, body(): pl.pallas_call(functools.partial(meet_kernel, rooms=rooms, lead=lead, cut...  24.4 us
    ppermute x12, starting transfers between devices, shifted(): return lax.ppermute(array, axis, [(i, (i + by) % n) for i in range(n)])  19.6 us
    pallas_call x1, Pallas kernels, finish(): pl.pallas_call(rest_kernel, name='rest_kernel', out_shape=[pltpu.HBM((per...  10.9 us
    pallas_call x1, Pallas kernels, finish(): plan, fs, ft, zs = make_plan(tzg, tfock, tfz, tzgt, ttrans, *tn, f, z)  5.88 us
    pallas_call x1, Pallas kernels, finish(): pl.pallas_call(w_kernel, name='w_kernel', out_shape=cut_tiles(per_cell),...  5.24 us
    cond x18, local copies, waits for them, and re-layouts  5.11 us
    pallas_call x1, Pallas kernels, finish(): pl.pallas_call(p_kernel, name='p_kernel', out_shape=[tiles(n) for n in (p...  4.63 us
  transfers between devices with their start and end apart: 12, of which 4 were waited for; matrix products, arithmetic and copies ran while one was open for 0% of the time, Pallas kernels for 22%

commit v1 on v0

--- a/solution.py
+++ b/solution.py
@@ -543,9 +543,7 @@
         compiler_params=params,
         cost_estimate=cost(2 * cap, 7 * per_cell),
     )(plan, ft, ws)
-    pn = []
-    for k, (axis, by) in enumerate(STEPS):
-        pn.append(shifted(p[k + 1], axis, -by))
+    pn = [shifted(p[k + 1], axis, -by) for k, (axis, by) in enumerate(STEPS)]
     fock_grad, part = pl.pallas_call(
         rest_kernel,
         name="rest_kernel",
@@ -568,7 +566,7 @@
 
 
 def rooms_of(per_cell, lead):
-    levels = ((29, 18, 12), (29, 18, 14), (30, 18, 13), (31, 18, 15), (34, 18, 17))
+    levels = ((30, 18, 12), (31, 18, 13), (31, 18, 14), (33, 18, 15), (36, 18, 17))
     scaled = [tuple(per_cell * room // 24 for room in level) for level in levels]
     return scaled + [(2 * per_cell - lead, per_cell, per_cell)]
 
@@ -580,10 +578,10 @@
     lists = (tasks_zg, tasks_fock, tasks_fz, tasks_zgt, tasks_trans)
     tzg, tfock, tfz, tzgt, ttrans = (t.reshape(t.shape[2], 1, t.shape[3]) for t in lists)
     a_list = jax.ShapeDtypeStruct(tzg.shape, I32)
-    lead = per_cell // 3
+    lead = per_cell // 4
     rooms = rooms_of(per_cell, lead)
     met = pl.pallas_call(
-        functools.partial(meet_kernel, rooms=rooms, lead=lead, cuts=lead // 4),
+        functools.partial(meet_kernel, rooms=rooms, lead=lead, cuts=lead // 3),
         name="meet_kernel",
         out_shape=[tiles(lead)] * 2
         + [a_list] * 4

time: 119 us -> 116 us (0.975)
  local copies, waits for them, and re-layouts: 5.13 us -> 0.04 us
  waiting for transfers between devices: 35.5 us -> 39.5 us
  Pallas kernels: 55.8 us -> 53.8 us
    cond x18 -> x6, local copies, waits for them, and re-layouts: 5.11 us -> 0.01 us
    ppermute x12, waiting for transfers between devices: 35.5 us -> 39.5 us  [shifted(): return lax.ppermute(array, axis, [(i, (i + by) % n) for i in range(n)])]
    pallas_call x1, Pallas kernels: 24.4 us -> 21.6 us  [body(): pl.pallas_call(functools.partial(meet_kernel, rooms=rooms, lead=lead, cut...]
  transfers between devices with their start and end apart: 12 -> 12, of which waited for: 4 -> 4; matrix products, arithmetic and copies ran while one was open for 0% -> 0% of each run, Pallas kernels for 22% -> 24%
where the time goes in v1:
time: 116 us
  Pallas kernels  53.8 us (46%)
  waiting for transfers between devices  39.5 us (34%)
  starting transfers between devices  19.9 us (17%)
  between operations  1.56 us (1%)
    ppermute x12, waiting for transfers between devices, shifted(): return lax.ppermute(array, axis, [(i, (i + by) % n) for i in range(n)])  39.5 us
    pallas_call x1, Pallas kernels, body(): pl.pallas_call(functools.partial(meet_kernel, rooms=rooms, lead=lead, cut...  21.6 us
    ppermute x12, starting transfers between devices, shifted(): return lax.ppermute(array, axis, [(i, (i + by) % n) for i in range(n)])  19.9 us
    pallas_call x1, Pallas kernels, finish(): pl.pallas_call(rest_kernel, name='rest_kernel', out_shape=[pltpu.HBM((per...  11.7 us
    pallas_call x1, Pallas kernels, finish(): plan, fs, ft, zs = make_plan(tzg, tfock, tfz, tzgt, ttrans, *tn, f, z)  5.88 us
    pallas_call x1, Pallas kernels, finish(): pl.pallas_call(w_kernel, name='w_kernel', out_shape=cut_tiles(per_cell),...  5.49 us
    pallas_call x1, Pallas kernels, finish(): pl.pallas_call(p_kernel, name='p_kernel', out_shape=[tiles(n) for n in (p...  4.64 us
    pallas_call x1, Pallas kernels, join(): pl.pallas_call(functools.partial(join_kernel, pieces=pieces), name='join_...  2.34 us
  transfers between devices with their start and end apart: 12, of which 4 were waited for; matrix products, arithmetic and copies ran while one was open for 0% of the time, Pallas kernels for 24%

profile of v1, /device:TPU:0, one launch (start us, length us, event | category | flops | bytes accessed | tf_op | source)
XLA Modules:
  0.0 115.6 jit_solution(13681616372023347037)
XLA Ops:
  0.7 21.6 %meet_kernel.1 = (f32[6,128,128]{2,1,0:T(8,128)S(1)}, f32[6,128,128]{2,1,0:T(8,128)S(1)}, s32[3,1,64]{2,1,0:T(1,128)S(1)}, s32[3,1,64]{2,1,0:T(1,128)S(1)}, s32[...) custom-call(s32[3,1,64]{2,1,0:T(1,128)} %bitcast.22, ...), custom_call_target="tpu_custom_call" | custom-call | tf_op jit(solution)/shard_map/meet_kernel/pallas_call | solution.py:583
  22.9 92.5 %conditional.1 = (f32[24,128,128]{2,1,0:T(8,128)}, f32[1,1,24,128,128]{4,3,2,1,0:T(8,128)}) conditional(s32[]{:T(128)} %bitcast.13, (s32[3,1,64]{2,1,0:T(1,128)S(1)}, s32[3,1,64]{2,1,0:T(1,128)S(1)}, s32[3,1,64]{2,1,0:T(1,128)S(1)}, s32[3,1,64]{2,1,0:T(1,128)S(1)}, s32[3,1,64]{2,1,0:T(1,128)S(1)}, ...), branch_computations={%region_0.0_spmd, %region_1.0_spmd, %region_2.0_spmd, %region_3.0_... | conditional | flops 15032385536 | bytes 213910320 | solution.py:615
  22.9 0.0 copy-start.40
  23.0 2.2 %pack_kernel.7 = (f32[13,128,128]{2,1,0:T(8,128)S(1)}, f32[13,128,128]{2,1,0:T(8,128)S(1)}) custom-call(s32[8,128]{1,0:T(8,128)S(1)} %get-tuple-element.254.pick, f32[24,128,128]{2,1,0:T(8,128)} %get-tuple-element.264.z.z0), custom_call_target="tpu_custom_call" | custom-call | bytes 6291456 | tf_op jit(solution)/shard_map/cond/branch_1_fun/pack_kernel/pallas_call | solution.py:510
  25.2 0.3 collective-permute-start.13
  25.4 0.3 collective-permute-start.12
  25.7 0.3 collective-permute-start.14
  26.0 5.0 %collective-permute-start.15 = (f32[18,128,128]{2,1,0:T(8,128)}, f32[18,128,128]{2,1,0:T(8,128)S(1)}, u32[]{:S(2)}, u32[]{:S(2)}) collective-permute-start(f32[18,128,128]{2,1,0:T(8,128)} %get-tuple-element.261), channel_id=1, source_target_pairs={{0,15},{1,0},{2,1},{3,2},{4,3},{5,4},{6,5},{7,6},{8,7},{9,8},{10,9... | collective-permute-start | bytes 3538952 | tf_op jit(solution)/shard_map/cond/branch_1_fun/ppermute | solution.py:465
  31.0 2.1 %collective-permute-start.17 = (f32[24,128,128]{2,1,0:T(8,128)}, f32[24,128,128]{2,1,0:T(8,128)S(1)}, u32[]{:S(2)}, u32[]{:S(2)}) collective-permute-start(f32[24,128,128]{2,1,0:T(8,128)} %get-tuple-element.264.z.z0), channel_id=1, source_target_pairs={{0,112},{16,0},{32,16},{48,32},{64,48},{80,64},{96,80},{112,96},{1... | collective-permute-start | bytes 4718600 | tf_op jit(solution)/shard_map/cond/branch_1_fun/ppermute | solution.py:465
  33.2 24.6 %collective-permute-done.14.g3 = f32[18,128,128]{2,1,0:T(8,128)S(1)} collective-permute-done((f32[18,128,128]{2,1,0:T(8,128)S(1)}, f32[18,128,128]{2,1,0:T(8,128)S(1)}, u32[]{:S(2)}, u32[]{:S(2)}) %collective-permute-start.14) | collective-permute-done | bytes 1179680 | tf_op jit(solution)/shard_map/cond/branch_1_fun/ppermute | solution.py:465
  57.7 0.0 collective-permute-start.16
  57.7 0.0 collective-permute-done.15.g4
  57.8 5.9 %plan_kernel.7 = (s32[32,128]{1,0:T(8,128)S(1)}, bf16[24,128,256]{2,1,0:T(8,128)(2,1)S(1)}, bf16[24,128,256]{2,1,0:T(8,128)(2,1)S(1)}, bf16[24,128,256]{2,1,0:T(8,128)(2,1)S(1)}) custom-call(s32[3,1,64]{2,1,0:T(1,128)S(1)} %get-tuple-element.242.tzg.tasks, s32[3,1,64]{2,1,0:T(1,128)S(1)} %get-tuple-element.239.tfock, ...), custom_call_target="tpu_custom_call" | custom-call | flops 2147483648 | bytes 12582912 | tf_op jit(solution)/shard_map/cond/branch_1_fun/plan_kernel/pallas_call | solution.py:525
  63.7 5.4 %collective-permute-start.19 = (f32[13,128,128]{2,1,0:T(8,128)S(1)}, f32[13,128,128]{2,1,0:T(8,128)S(1)}, u32[]{:S(2)}, u32[]{:S(2)}) collective-permute-start(f32[13,128,128]{2,1,0:T(8,128)S(1)} %get-tuple-element.266), channel_id=1, source_target_pairs={{0,15},{1,0},{2,1},{3,2},{4,3},{5,4},{6,5},{7,6},{8,7},{9,8},{10,9... | collective-permute-start | bytes 2555912 | tf_op jit(solution)/shard_map/cond/branch_1_fun/ppermute | solution.py:465
  69.1 5.5 %w_kernel.7.ws = bf16[24,128,256]{2,1,0:T(8,128)(2,1)S(1)} custom-call(s32[3,1,64]{2,1,0:T(1,128)S(1)} %get-tuple-element.242.tzg.tasks, s32[32,128]{1,0:T(8,128)S(1)} %get-tuple-element.250.plan, bf16[24,128,256]{2,1,0:T(8,128)(2,1)S(1)} %get-tuple-element.252.zs, f32[24,128,128]{2,1,0:T(8,128)} %get-tuple-element.257.g0, ...), custom_call_target="tpu_custom_call" | custom-call | flops 2147483648 | bytes 11010048 | tf_op jit(solution)/shard_map/cond/branch_1_fun/w_kernel/pallas_call | solution.py:526
  74.6 4.6 %p_kernel.7 = (f32[24,128,128]{2,1,0:T(8,128)S(1)}, f32[18,128,128]{2,1,0:T(8,128)S(1)}, f32[18,128,128]{2,1,0:T(8,128)S(1)}, f32[13,128,128]{2,1,0:T(8,128)S(1)}, f32[13,128,128]{2,1,0:T(8,128)S(1)}) custom-call(s32[32,128]{1,0:T(8,128)S(1)} %get-tuple-element.250.plan, bf16[24,128,256]{2,1,0:T(8,128)(2,1)S(1)} %get-tuple-element.262.ft, ...), custom_call_target="tpu_custom_call" | custom-call | flops 4294967296 | bytes 11010048 | tf_op jit(solution)/shard_map/cond/branch_1_fun/p_kernel/pallas_call | solution.py:536
  79.2 0.0 collective-permute-start.20
  79.2 3.4 %collective-permute-done.18.z3 = f32[13,128,128]{2,1,0:T(8,128)S(1)} collective-permute-done((f32[13,128,128]{2,1,0:T(8,128)S(1)}, f32[13,128,128]{2,1,0:T(8,128)S(1)}, u32[]{:S(2)}, u32[]{:S(2)}) %collective-permute-start.18) | collective-permute-done | bytes 852000 | tf_op jit(solution)/shard_map/cond/branch_1_fun/ppermute | solution.py:465
  82.6 0.7 collective-permute-start.21
  83.3 4.5 %collective-permute-done.19.z4 = f32[13,128,128]{2,1,0:T(8,128)S(1)} collective-permute-done((f32[13,128,128]{2,1,0:T(8,128)S(1)}, f32[13,128,128]{2,1,0:T(8,128)S(1)}, u32[]{:S(2)}, u32[]{:S(2)}) %collective-permute-start.19) | collective-permute-done | bytes 852000 | tf_op jit(solution)/shard_map/cond/branch_1_fun/ppermute | solution.py:465
  87.9 5.8 %collective-permute-start.23 = (f32[13,128,128]{2,1,0:T(8,128)S(1)}, f32[13,128,128]{2,1,0:T(8,128)S(1)}, u32[]{:S(2)}, u32[]{:S(2)}) collective-permute-start(f32[13,128,128]{2,1,0:T(8,128)S(1)} %get-tuple-element.272), channel_id=1, source_target_pairs={{0,15},{1,0},{2,1},{3,2},{4,3},{5,4},{6,5},{7,6},{8,7},{9,8},{10,9... | collective-permute-start | bytes 2555912 | tf_op jit(solution)/shard_map/cond/branch_1_fun/ppermute | solution.py:465
  93.7 11.7 %rest_kernel.7 = (f32[24,128,128]{2,1,0:T(8,128)}, f32[24,128,128]{2,1,0:T(8,128)S(1)}) custom-call(s32[3,1,64]{2,1,0:T(1,128)S(1)} %get-tuple-element.239.tfock, s32[3,1,64]{2,1,0:T(1,128)S(1)} %get-tuple-element.240.tfz, s32[3,1,64]{2,1,0:T(1,128)S(1)} %get-tuple-element.241.tzgt, s32[32,128]{1,0:T(8,128)S(1)} %get-tuple-element.250.plan, ...), custom_call_target="tpu_custom_call" | custom-call | flops 6442450944 | bytes 22020096 | tf_op jit(solution)/shard_map/cond/branch_1_fun/rest_kernel/pallas_call | solution.py:547
  105.3 7.0 %collective-permute-done.22.p3 = f32[13,128,128]{2,1,0:T(8,128)S(1)} collective-permute-done((f32[13,128,128]{2,1,0:T(8,128)S(1)}, f32[13,128,128]{2,1,0:T(8,128)S(1)}, u32[]{:S(2)}, u32[]{:S(2)}) %collective-permute-start.22) | collective-permute-done | bytes 852000 | tf_op jit(solution)/shard_map/cond/branch_1_fun/ppermute | solution.py:465
  112.4 2.3 %join_kernel.7 = f32[24,128,128]{2,1,0:T(8,128)} custom-call(s32[32,128]{1,0:T(8,128)S(1)} %get-tuple-element.250.plan, f32[24,128,128]{2,1,0:T(8,128)S(1)} %get-tuple-element.268.part, f32[18,128,128]{2,1,0:T(8,128)S(1)} %collective-permute-done.20.p1, f32[18,128,128]{2,1,0:T(8,128)S(1)} %collective-permute-done.21.p2, ...), custom_call_target="tpu_custom_call" | custom-call | bytes 6291456 | tf_op jit(solution)/shard_map/cond/branch_1_fun/join_kernel/pallas_call | solution.py:479
  (24 shorter events, 0.1 us)
Async XLA Ops:
  0.6 22.2 %copy-start.34 = (s32[1,1,3,64]{3,1,2,0:T(1,128)S(1)}, s32[1,1,3,64]{3,1,2,0:T(1,128)}, u32[]{:S(2)}) copy-start(s32[1,1,3,64]{3,1,2,0:T(1,128)} %param.17) | copy-start | bytes 2308
  0.6 22.2 %copy-start.35 = (s32[1,1,3,64]{3,1,2,0:T(1,128)S(1)}, s32[1,1,3,64]{3,1,2,0:T(1,128)}, u32[]{:S(2)}) copy-start(s32[1,1,3,64]{3,1,2,0:T(1,128)} %param.18) | copy-start | bytes 2308
  0.7 22.2 %copy-start.36 = (s32[1,1,3,64]{3,1,2,0:T(1,128)S(1)}, s32[1,1,3,64]{3,1,2,0:T(1,128)}, u32[]{:S(2)}) copy-start(s32[1,1,3,64]{3,1,2,0:T(1,128)} %param.19) | copy-start | bytes 2308
  0.7 22.2 %copy-start.37 = (s32[1,1,3,64]{3,1,2,0:T(1,128)S(1)}, s32[1,1,3,64]{3,1,2,0:T(1,128)}, u32[]{:S(2)}) copy-start(s32[1,1,3,64]{3,1,2,0:T(1,128)} %param.20) | copy-start | bytes 2308
  0.7 22.2 %copy-start.38 = (s32[1,1,3,64]{3,1,2,0:T(1,128)S(1)}, s32[1,1,3,64]{3,1,2,0:T(1,128)}, u32[]{:S(2)}) copy-start(s32[1,1,3,64]{3,1,2,0:T(1,128)} %param.21) | copy-start | bytes 2308
  22.9 34.8 %copy-start.40 = (f32[24,128,128]{2,1,0:T(8,128)S(1)}, f32[24,128,128]{2,1,0:T(8,128)}, u32[]{:S(2)}) copy-start(f32[24,128,128]{2,1,0:T(8,128)} %get-tuple-element.248.f) | copy-start | bytes 4718596 | tf_op jit(solution)/shard_map/cond
  25.2 38.5 %collective-permute-start.13 = (f32[24,128,128]{2,1,0:T(8,128)}, f32[24,128,128]{2,1,0:T(8,128)S(1)}, u32[]{:S(2)}, u32[]{:S(2)}) collective-permute-start(f32[24,128,128]{2,1,0:T(8,128)} %get-tuple-element.257.g0), channel_id=1, source_target_pairs={{0,112},{16,0},{32,16},{48,32},{64,48},{80,64},{96,80},{112,96},{1... | collective-permute-start | bytes 4718600 | tf_op jit(solution)/shard_map/cond/branch_1_fun/ppermute | solution.py:465
  25.4 43.6 %collective-permute-start.12 = (f32[24,128,128]{2,1,0:T(8,128)}, f32[24,128,128]{2,1,0:T(8,128)S(1)}, u32[]{:S(2)}, u32[]{:S(2)}) collective-permute-start(f32[24,128,128]{2,1,0:T(8,128)} %get-tuple-element.257.g0), channel_id=1, source_target_pairs={{0,16},{16,32},{32,48},{48,64},{64,80},{80,96},{96,112},{112,0},{1... | collective-permute-start | bytes 4718600 | tf_op jit(solution)/shard_map/cond/branch_1_fun/ppermute | solution.py:465
  25.7 32.0 %collective-permute-start.14 = (f32[18,128,128]{2,1,0:T(8,128)S(1)}, f32[18,128,128]{2,1,0:T(8,128)S(1)}, u32[]{:S(2)}, u32[]{:S(2)}) collective-permute-start(f32[18,128,128]{2,1,0:T(8,128)S(1)} %get-tuple-element.259), channel_id=1, source_target_pairs={{0,1},{1,2},{2,3},{3,4},{4,5},{5,6},{6,7},{7,8},{8,9},{9,10},{10,1... | collective-permute-start | bytes 3538952 | tf_op jit(solution)/shard_map/cond/branch_1_fun/ppermute | solution.py:465
  26.0 31.7 %collective-permute-start.15 = (f32[18,128,128]{2,1,0:T(8,128)}, f32[18,128,128]{2,1,0:T(8,128)S(1)}, u32[]{:S(2)}, u32[]{:S(2)}) collective-permute-start(f32[18,128,128]{2,1,0:T(8,128)} %get-tuple-element.261), channel_id=1, source_target_pairs={{0,15},{1,0},{2,1},{3,2},{4,3},{5,4},{6,5},{7,6},{8,7},{9,8},{10,9... | collective-permute-start | bytes 3538952 | tf_op jit(solution)/shard_map/cond/branch_1_fun/ppermute | solution.py:465
  31.0 56.8 %collective-permute-start.17 = (f32[24,128,128]{2,1,0:T(8,128)}, f32[24,128,128]{2,1,0:T(8,128)S(1)}, u32[]{:S(2)}, u32[]{:S(2)}) collective-permute-start(f32[24,128,128]{2,1,0:T(8,128)} %get-tuple-element.264.z.z0), channel_id=1, source_target_pairs={{0,112},{16,0},{32,16},{48,32},{64,48},{80,64},{96,80},{112,96},{1... | collective-permute-start | bytes 4718600 | tf_op jit(solution)/shard_map/cond/branch_1_fun/ppermute | solution.py:465
  57.7 35.9 %collective-permute-start.16 = (f32[24,128,128]{2,1,0:T(8,128)}, f32[24,128,128]{2,1,0:T(8,128)S(1)}, u32[]{:S(2)}, u32[]{:S(2)}) collective-permute-start(f32[24,128,128]{2,1,0:T(8,128)} %get-tuple-element.264.z.z0), channel_id=1, source_target_pairs={{0,16},{16,32},{32,48},{48,64},{64,80},{80,96},{96,112},{112,0},{1... | collective-permute-start | bytes 4718600 | tf_op jit(solution)/shard_map/cond/branch_1_fun/ppermute | solution.py:465
  57.7 24.9 %collective-permute-start.18 = (f32[13,128,128]{2,1,0:T(8,128)S(1)}, f32[13,128,128]{2,1,0:T(8,128)S(1)}, u32[]{:S(2)}, u32[]{:S(2)}) collective-permute-start(f32[13,128,128]{2,1,0:T(8,128)S(1)} %get-tuple-element.265), channel_id=1, source_target_pairs={{0,1},{1,2},{2,3},{3,4},{4,5},{5,6},{6,7},{7,8},{8,9},{9,10},{10,1... | collective-permute-start | bytes 2555912 | tf_op jit(solution)/shard_map/cond/branch_1_fun/ppermute | solution.py:465
  63.6 10.9 %copy-start.1 = (f32[24,128,128]{2,1,0:T(8,128)}, f32[24,128,128]{2,1,0:T(8,128)S(1)}, u32[]{:S(2)}) copy-start(f32[24,128,128]{2,1,0:T(8,128)S(1)} %collective-permute-done.13.g2) | copy-start | bytes 4718596 | tf_op jit(solution)/shard_map/cond
  63.7 24.2 %collective-permute-start.19 = (f32[13,128,128]{2,1,0:T(8,128)S(1)}, f32[13,128,128]{2,1,0:T(8,128)S(1)}, u32[]{:S(2)}, u32[]{:S(2)}) collective-permute-start(f32[13,128,128]{2,1,0:T(8,128)S(1)} %get-tuple-element.266), channel_id=1, source_target_pairs={{0,15},{1,0},{2,1},{3,2},{4,3},{5,4},{6,5},{7,6},{8,7},{9,8},{10,9... | collective-permute-start | bytes 2555912 | tf_op jit(solution)/shard_map/cond/branch_1_fun/ppermute | solution.py:465
  69.1 5.5 %copy-start.6 = (f32[24,128,128]{2,1,0:T(8,128)}, f32[24,128,128]{2,1,0:T(8,128)S(1)}, u32[]{:S(2)}) copy-start(f32[24,128,128]{2,1,0:T(8,128)S(1)} %collective-permute-done.12.g1) | copy-start | bytes 4718596 | tf_op jit(solution)/shard_map/cond
  79.2 33.1 %collective-permute-start.20 = (f32[18,128,128]{2,1,0:T(8,128)S(1)}, f32[18,128,128]{2,1,0:T(8,128)S(1)}, u32[]{:S(2)}, u32[]{:S(2)}) collective-permute-start(f32[18,128,128]{2,1,0:T(8,128)S(1)} %get-tuple-element.269), channel_id=1, source_target_pairs={{0,16},{16,32},{32,48},{48,64},{64,80},{80,96},{96,112},{112,0},{1... | collective-permute-start | bytes 3538952 | tf_op jit(solution)/shard_map/cond/branch_1_fun/ppermute | solution.py:465
  82.6 29.7 %collective-permute-start.21 = (f32[18,128,128]{2,1,0:T(8,128)S(1)}, f32[18,128,128]{2,1,0:T(8,128)S(1)}, u32[]{:S(2)}, u32[]{:S(2)}) collective-permute-start(f32[18,128,128]{2,1,0:T(8,128)S(1)} %get-tuple-element.270), channel_id=1, source_target_pairs={{0,112},{16,0},{32,16},{48,32},{64,48},{80,64},{96,80},{112,96},{1... | collective-permute-start | bytes 3538952 | tf_op jit(solution)/shard_map/cond/branch_1_fun/ppermute | solution.py:465
  87.9 24.5 %collective-permute-start.22 = (f32[13,128,128]{2,1,0:T(8,128)S(1)}, f32[13,128,128]{2,1,0:T(8,128)S(1)}, u32[]{:S(2)}, u32[]{:S(2)}) collective-permute-start(f32[13,128,128]{2,1,0:T(8,128)S(1)} %get-tuple-element.271), channel_id=1, source_target_pairs={{0,1},{1,2},{2,3},{3,4},{4,5},{5,6},{6,7},{7,8},{8,9},{9,10},{10,1... | collective-permute-start | bytes 2555912 | tf_op jit(solution)/shard_map/cond/branch_1_fun/ppermute | solution.py:465
  87.9 24.5 %collective-permute-start.23 = (f32[13,128,128]{2,1,0:T(8,128)S(1)}, f32[13,128,128]{2,1,0:T(8,128)S(1)}, u32[]{:S(2)}, u32[]{:S(2)}) collective-permute-start(f32[13,128,128]{2,1,0:T(8,128)S(1)} %get-tuple-element.272), channel_id=1, source_target_pairs={{0,15},{1,0},{2,1},{3,2},{4,3},{5,4},{6,5},{7,6},{8,7},{9,8},{10,9... | collective-permute-start | bytes 2555912 | tf_op jit(solution)/shard_map/cond/branch_1_fun/ppermute | solution.py:465
